TPU v7x, 32 devices: a whole 2x2x4 slice. The times are simulated.
32 devices in a mesh: dp: 16 (over z, x, core), tensor: 2 (over y).
Axes of the slice: x: 2, y: 2, z: 4, core: 2. Of those that a mesh axis runs over, the one named last changes fastest.
Arguments:
- x_in: bfloat16 [16384, 2048], P('dp'), may hold values from -6 to 6
- norm_gain: float32 [2048], replicated, may hold values from 0.5 to 1.5
- w_zx: bfloat16 [2048, 2, 4096], P(None, None, 'tensor'), may hold values from -0.125 to 0.125
- w_bc: bfloat16 [2048, 256], replicated, may hold values from -0.125 to 0.125
- w_dt: bfloat16 [2048, 64], P(None, 'tensor'), may hold values from -0.125 to 0.125
- conv_x: float32 [5, 4096], P(None, 'tensor'), may hold values from -3 to 3
- conv_bc: float32 [5, 256], replicated, may hold values from -3 to 3
- dt_bias: float32 [64], P('tensor'), may hold values from -4 to -1
- a_log: float32 [64], P('tensor'), may hold values from -3 to 1.5
- d_skip: float32 [64], P('tensor'), may hold values from 0.5 to 1.5
- gate_gain: float32 [4096], P('tensor'), may hold values from 0.5 to 1.5
- w_out: bfloat16 [4096, 2048], P('tensor'), may hold values from -0.09375 to 0.09375
- cotangent: bfloat16 [16384, 2048], P('dp'), may hold values from -6 to 6
- block_parent: int32 [128], P('dp'), may hold values from -1 to 6, as said below
Outputs:
- mixed: bfloat16 [16384, 2048], P('dp')
- input_grad: bfloat16 [16384, 2048], P('dp')
- norm_gain_grad: float32 [2048], replicated
- w_zx_grad: float32 [2048, 2, 4096], P('dp', None, 'tensor')
- w_bc_grad: float32 [2048, 256], replicated
- w_dt_grad: float32 [2048, 64], P('dp', 'tensor')
- conv_x_grad: float32 [5, 4096], P(None, 'tensor')
- conv_bc_grad: float32 [5, 256], replicated
- dt_bias_grad: float32 [64], P('tensor')
- a_log_grad: float32 [64], P('tensor')
- d_skip_grad: float32 [64], P('tensor')
- gate_gain_grad: float32 [4096], P('tensor')
- w_out_grad: float32 [4096, 2048], P('tensor', 'dp')
Inputs may be any that keep to these rules, and one draw needn't show every extreme that they name: `block_parent`: each device's 8 blocks hold one tree. A block's entry is the index, among its device's blocks, of an earlier block whose last token precedes its first token, or -1 at the root; the first half of the blocks or more form a chain from the root, and the last block continues the block before it.
All inputs are finite; a program needn't handle non-finite values.
Results may differ from a plain program's by a relative error of at most 0.014.
Values may be sent and summed in bfloat16 or wider, within the bound.
No kernel may reach another device: no remote copies, remote signals or barrier semaphores. Data moves between devices by JAX's collectives and lax.ppermute only.
A program may use at most 320 MiB of HBM per device.

v0:
```python
import jax
import jax.numpy as jnp
from jax import lax
from jax.sharding import PartitionSpec as P

epsilon = 1e-05
highest = lax.Precision.HIGHEST


def conv_path(inputs, kernel, parent):
    blocks = parent.shape[0]
    tokens, channels = inputs.shape
    window = kernel.shape[0] - 1
    block_len = tokens // blocks
    blocked = inputs.reshape(blocks, block_len, channels)
    trailing = blocked[:, block_len - (window - 1) :, :]
    context = jnp.take(trailing, jnp.maximum(parent, 0), axis=0)
    context = jnp.where((parent >= 0)[:, None, None], context, jnp.zeros_like(context))
    padded = jnp.concatenate([context, blocked], axis=1)
    summed = kernel[window][None, None, :] + jnp.zeros_like(blocked)
    for offset in range(window):
        summed = summed + kernel[offset][None, None, :] * padded[:, offset : offset + block_len, :]
    return jax.nn.silu(summed).reshape(tokens, channels)


def decay_paths(block_decay, parent):
    blocks = parent.shape[0]
    n_heads = block_decay.shape[1]
    parent_map = (parent[:, None] == jnp.arange(blocks, dtype=jnp.int32)[None, :]).astype(
        jnp.float32
    )
    identity = jnp.eye(blocks, dtype=jnp.float32)

    def advance(turn, paths):
        return identity[None] + jnp.einsum(
            "hb,bp,hpa->hba", block_decay.T, parent_map, paths, precision=highest
        )

    paths = lax.fori_loop(0, blocks, advance, jnp.broadcast_to(identity, (n_heads, blocks, blocks)))
    return (paths, parent_map)


def ssd_mix(x_heads, b_rows, c_rows, dt_raw, dt_bias, a_log, d_skip, parent):
    tokens, n_heads, head_dim = x_heads.shape
    blocks = parent.shape[0]
    block_len = tokens // blocks
    dt_values = jax.nn.softplus(dt_raw + dt_bias)
    log_rate = dt_values * -jnp.exp(a_log)
    x_blocks = x_heads.reshape(blocks, block_len, n_heads, head_dim)
    b_blocks = b_rows.reshape(blocks, block_len, -1)
    c_blocks = c_rows.reshape(blocks, block_len, -1)
    dt_blocks = dt_values.reshape(blocks, block_len, n_heads)
    cumulant = jnp.cumsum(log_rate.reshape(blocks, block_len, n_heads), axis=1)
    scores = jnp.einsum("bin,bjn->bij", c_blocks, b_blocks, precision=highest)
    rows_idx = jnp.arange(block_len, dtype=jnp.int32)
    causal = (rows_idx[:, None] >= rows_idx[None, :])[None, :, :, None]
    log_gap = cumulant[:, :, None, :] - cumulant[:, None, :, :]
    decays = jnp.where(causal, jnp.exp(jnp.where(causal, log_gap, 0.0)), 0.0)
    weights = scores[..., None] * decays * dt_blocks[:, None, :, :]
    within = jnp.einsum("bijh,bjhp->bihp", weights, x_blocks, precision=highest)
    to_end = jnp.exp(cumulant[:, -1:, :] - cumulant) * dt_blocks
    local_states = jnp.einsum("bjh,bjhp,bjn->bhpn", to_end, x_blocks, b_blocks, precision=highest)
    paths, parent_map = decay_paths(jnp.exp(cumulant[:, -1, :]), parent)
    end_states = jnp.einsum("hba,ahpn->bhpn", paths, local_states, precision=highest)
    start_states = jnp.einsum("bq,qhpn->bhpn", parent_map, end_states, precision=highest)
    carried = jnp.exp(cumulant)[..., None] * jnp.einsum(
        "bin,bhpn->bihp", c_blocks, start_states, precision=highest
    )
    result = within + carried + d_skip[None, None, :, None] * x_blocks
    return result.reshape(tokens, n_heads * head_dim)


def gated_mix(x_heads, bc_rows, dt_raw, dt_bias, a_log, d_skip, z_gate, parent):
    half = bc_rows.shape[1] // 2
    mixed_heads = ssd_mix(
        x_heads, bc_rows[:, :half], bc_rows[:, half:], dt_raw, dt_bias, a_log, d_skip, parent
    )
    return mixed_heads * jax.nn.silu(z_gate)


def over_tokens(left, right):
    return lax.dot_general(
        left, right, (((0,), (0,)), ((), ())), preferred_element_type=jnp.float32
    )


def over_columns(left, right):
    return lax.dot_general(
        left, right, (((1,), (1,)), ((), ())), preferred_element_type=jnp.float32
    )


def rounded(value):
    return lax.optimization_barrier(value.astype(jnp.bfloat16)).astype(jnp.float32)


def local(
    x_in,
    norm_gain,
    w_zx,
    w_bc,
    w_dt,
    conv_x,
    conv_bc,
    dt_bias,
    a_log,
    d_skip,
    gate_gain,
    w_out,
    cotangent,
    block_parent,
):
    tokens, features = x_in.shape
    local_heads = w_dt.shape[1]
    inner_width = w_zx.shape[2]
    head_dim = inner_width // local_heads
    full_width = inner_width * lax.axis_size("tensor")
    x_float = x_in.astype(jnp.float32)
    inv_rms = lax.rsqrt(jnp.mean(x_float * x_float, axis=-1) + epsilon)
    normed = (x_float * inv_rms[:, None] * norm_gain).astype(jnp.bfloat16)
    z_gate = jnp.dot(normed, w_zx[:, 0, :], preferred_element_type=jnp.float32)
    x_pre = jnp.dot(normed, w_zx[:, 1, :], preferred_element_type=jnp.float32)
    bc_pre = jnp.dot(normed, w_bc, preferred_element_type=jnp.float32)
    dt_raw = jnp.dot(normed, w_dt, preferred_element_type=jnp.float32)

    def x_piece(values, kernel):
        return conv_path(values, kernel, block_parent)

    x_conv, x_pull = jax.vjp(x_piece, x_pre, conv_x)
    bc_conv, bc_pull = jax.vjp(x_piece, bc_pre, conv_bc)
    x_round = rounded(x_conv)
    bc_round = rounded(bc_conv)

    def mixer(x_values, bc_values, dt_values, bias_values, log_values, skip_values, gate_values):
        return gated_mix(
            x_values.reshape(tokens, local_heads, head_dim),
            bc_values,
            dt_values,
            bias_values,
            log_values,
            skip_values,
            gate_values,
            block_parent,
        )

    gated, mix_pull = jax.vjp(mixer, x_round, bc_round, dt_raw, dt_bias, a_log, d_skip, z_gate)
    squares = lax.psum(jnp.sum(gated * gated, axis=-1), "tensor")
    inv_gate = lax.rsqrt(squares / full_width + epsilon)
    gate_normed = (gated * inv_gate[:, None] * gate_gain).astype(jnp.bfloat16)
    partial_out = jnp.dot(gate_normed, w_out, preferred_element_type=jnp.float32)
    share = tokens // lax.axis_size("tensor")
    first_row = lax.axis_index("tensor") * share
    x_rows = lax.dynamic_slice_in_dim(x_float, first_row, share, 0)
    mixed = (
        x_float + lax.psum(partial_out.astype(jnp.bfloat16), "tensor").astype(jnp.float32)
    ).astype(jnp.bfloat16)
    d_gate_normed = over_columns(cotangent, w_out)
    w_out_part = over_tokens(gate_normed, cotangent)
    gate_gain_part = jnp.sum(d_gate_normed * gated * inv_gate[:, None], axis=0)
    scaled = d_gate_normed * gate_gain
    cross = lax.psum(jnp.sum(scaled * gated, axis=-1), "tensor")
    d_gated = (
        inv_gate[:, None] * scaled
        - gated * (inv_gate * inv_gate * inv_gate * cross / full_width)[:, None]
    )
    d_x_round, d_bc_round, d_dt_raw, dt_bias_part, a_log_part, d_skip_part, d_z_gate = mix_pull(
        d_gated
    )
    d_x_pre, conv_x_part = x_pull(d_x_round)
    d_bc_pre, conv_bc_part = bc_pull(d_bc_round)
    z_low = d_z_gate.astype(jnp.bfloat16)
    x_low = d_x_pre.astype(jnp.bfloat16)
    bc_low = d_bc_pre.astype(jnp.bfloat16)
    dt_low = d_dt_raw.astype(jnp.bfloat16)
    w_zx_part = jnp.stack([over_tokens(normed, z_low), over_tokens(normed, x_low)], axis=1)
    w_bc_part = over_tokens(normed, bc_low)
    w_dt_part = over_tokens(normed, dt_low)
    d_normed = over_columns(z_low, w_zx[:, 0, :]) + over_columns(x_low, w_zx[:, 1, :])
    d_normed = d_normed + over_columns(bc_low, w_bc) + over_columns(dt_low, w_dt)
    norm_gain_part = jnp.sum(d_normed * x_float * inv_rms[:, None], axis=0)
    d_rows = lax.psum_scatter(
        d_normed.astype(jnp.bfloat16), "tensor", scatter_dimension=0, tiled=True
    ).astype(jnp.float32)
    rms_rows = lax.dynamic_slice_in_dim(inv_rms, first_row, share, 0)
    cot_rows = lax.dynamic_slice_in_dim(cotangent, first_row, share, 0).astype(jnp.float32)
    gained = d_rows * norm_gain
    spread = rms_rows * rms_rows * rms_rows * jnp.sum(gained * x_rows, axis=-1) / features
    d_input = cot_rows + rms_rows[:, None] * gained - x_rows * spread[:, None]
    input_grad = lax.all_gather(d_input.astype(jnp.bfloat16), "tensor", axis=0, tiled=True)
    w_zx_grad, w_dt_grad, w_out_grad = (
        lax.psum_scatter(
            w_zx_part.astype(jnp.bfloat16), "dp", scatter_dimension=0, tiled=True
        ).astype(jnp.float32),
        lax.psum_scatter(
            w_dt_part.astype(jnp.bfloat16), "dp", scatter_dimension=0, tiled=True
        ).astype(jnp.float32),
        lax.psum_scatter(
            w_out_part.astype(jnp.bfloat16), "dp", scatter_dimension=1, tiled=True
        ).astype(jnp.float32),
    )
    conv_x_grad, dt_bias_grad, a_log_grad, d_skip_grad, gate_gain_grad = lax.psum(
        (conv_x_part, dt_bias_part, a_log_part, d_skip_part, gate_gain_part), "dp"
    )
    norm_gain_grad, w_bc_grad, conv_bc_grad = lax.psum(
        (norm_gain_part, w_bc_part, conv_bc_part), ("dp", "tensor")
    )
    return (
        mixed,
        input_grad,
        norm_gain_grad,
        w_zx_grad,
        w_bc_grad,
        w_dt_grad,
        conv_x_grad,
        conv_bc_grad,
        dt_bias_grad,
        a_log_grad,
        d_skip_grad,
        gate_gain_grad,
        w_out_grad,
    )


def solution(mesh):
    return jax.shard_map(
        local,
        mesh=mesh,
        in_specs=(
            P("dp", None),
            P(),
            P(None, None, "tensor"),
            P(),
            P(None, "tensor"),
            P(None, "tensor"),
            P(),
            P("tensor"),
            P("tensor"),
            P("tensor"),
            P("tensor"),
            P("tensor", None),
            P("dp", None),
            P("dp"),
        ),
        out_specs=(
            P("dp", None),
            P("dp", None),
            P(),
            P("dp", None, "tensor"),
            P(),
            P("dp", "tensor"),
            P(None, "tensor"),
            P(),
            P("tensor"),
            P("tensor"),
            P("tensor"),
            P("tensor"),
            P("tensor", "dp"),
        ),
        check_vma=False,
    )
```

profile of v0, /device:TPU:0, one launch (start us, length us, event | category | flops | bytes accessed | tf_op | source)
XLA Modules:
  0.0 1176.5 jit_solution(15319442505596880165)
XLA Ops:
  12.6 32.8 %fusion.165 = (bf16[2048,1,2048]{2,1,0:T(2,128)(2,1)}, bf16[2048,1,2048]{2,1,0:T(2,128)(2,1)}) fusion(bf16[2048,2,2048]{2,1,0:T(2,128)(2,1)} %param.20), kind=kLoop, calls=%fused_computation.254 | loop fusion | bytes 33554432 | tf_op jit(solution)/shard_map/slice | solution.py:121
  46.5 13.6 %fusion.40 = f32[8,128,2048]{2,1,0:T(8,128)S(1)} fusion(bf16[8,128,2048]{2,1,0:T(8,128)(2,1)S(1)} %bitcast.263, bf16[2048,1,2048]{2,1,0:T(2,128)(2,1)} %get-tuple-element.380), kind=kOutput, calls=%fused_computation.63 | convolution fusion | flops 8589934592 | bytes 20971520 | tf_op jit(solution)/shard_map/dot_general | solution.py:122
  64.3 16.3 %multiply_convert_fusion.1 = (bf16[8,128,2048]{2,1,0:T(8,128)(2,1)}, f32[8,128,2048]{2,1,0:T(8,128)}) fusion(f32[8,128,2048]{2,1,0:T(8,128)} %copy-done.7, f32[2048]{0:T(1024)S(1)} %bitcast.305, f32[8,3,2048]{2,1,0:T(4,128)S(1)} %select_select_fusion, f32[2048]{0:T(1024)S(1)} %bitcast.307, f32[2048]{0:T(1024)S(1)} %bitcast.301, f32[2048]{0:T(1024)S(1)} %bitcast.303, ...), kind=kLoop, calls=%fused_computation.101 | loop fusion | flops 33554432 | bytes 21209088 | tf_op jit(solution)/shard_map/convert_element_type | solution.py:94
  80.6 13.3 %reshape.279 = f32[8,128,32,64]{3,2,1,0:T(8,128)} reshape(bf16[1024,2048]{1,0:T(8,128)(2,1)} %bitcast.260) | data formatting | bytes 12582912 | tf_op jit(solution)/shard_map/jvp()/reshape;jvp()/reshape | solution.py:49
  104.8 23.3 %fusion.171 = f32[8,128,32]{2,0,1:T(8,128)S(1)} fusion(f32[8,128,32]{2,0,1:T(8,128)S(1)} %copy.143), kind=kOutput, calls=%fused_computation.260 | output fusion | flops 4161536 | bytes 262144 | tf_op jit(solution)/shard_map/jvp(jit(cumsum))/reduce_window_sum | solution.py:53
  130.3 14.9 %copy.158 = f32[8,128,32,64]{1,3,2,0:T(8,128)} copy(f32[8,128,32,64]{3,2,1,0:T(8,128)} %reshape.279) | data formatting | bytes 16777216 | tf_op jit(solution)/shard_map/jvp()/reshape;jvp()/reshape | solution.py:49
  161.8 9.1 while.30
  170.9 7.6 fusion.48
  178.5 13.6 %fusion.73 = f32[32,64,128,8]{2,3,1,0:T(8,128)S(1)} fusion(f32[8,32,64,128]{3,2,1,0:T(8,128)S(1)} %fusion.48, f32[32,8,8]{2,1,0:T(8,128)S(1)} %get-tuple-element.163), kind=kOutput, calls=%fused_computation.120 | convolution fusion | flops 201326592 | bytes 16785408 | tf_op jit(solution)/shard_map/jvp(hba,ahpn->bhpn)/dot_general | solution.py:64
  198.5 9.5 fusion.69
  211.3 21.9 %fusion.39 = f32[8,128,32,64]{1,3,2,0:T(8,128)} fusion(f32[8,128,32,64]{1,3,2,0:T(8,128)} %copy.158, f32[8,128,32,64]{1,3,2,0:T(8,128)S(1)} %fusion.69, f32[32]{0:T(128)S(1)} %copy-done.90, f32[8,128,32]{1,2,0:T(8,128)S(1)} %copy.148, f32[8,128,32]{1,2,0:T(8,128)S(1)} %bitcast.298, f32[8,128,32]{1,2,0:T(8,128)S(1)} %copy-done.36, ...), kind=kOutput, calls=%fused_computation.62 | convolution fusion | flops 3250585600 | bytes 30294144 | tf_op jit(solution)/shard_map/jvp(bijh,bjhp->bihp)/dot_general | solution.py:60
  233.2 16.2 %copy.215 = f32[8,128,32,64]{3,2,1,0:T(8,128)} copy(f32[8,128,32,64]{1,3,2,0:T(8,128)} %fusion.39) | data formatting | bytes 16777216 | tf_op jit(solution)/shard_map/jvp()/reshape | solution.py:70
  249.4 14.8 %reshape.284 = f32[1024,2048]{1,0:T(8,128)} reshape(f32[8,128,32,64]{3,2,1,0:T(8,128)} %copy.215) | data formatting | bytes 16777216 | tf_op jit(solution)/shard_map/jvp()/reshape | solution.py:70
  264.3 19.7 %multiply_reduce_fusion.11 = (f32[1024]{0:T(1024)S(1)}, f32[1024,2048]{1,0:T(8,128)}, f32[1024,2048]{1,0:T(8,128)}) fusion(f32[1024,2048]{1,0:T(8,128)} %reshape.284, bf16[1024,2048]{1,0:T(8,128)(2,1)} %copy-done.2, bf16[2048,1,2048]{2,1,0:T(2,128)(2,1)} %get-tuple-element.379), kind=kOutput, calls=%fused_computation.85 | convolution fusion | flops 8604613632 | bytes 37752832 | tf_op jit(solution)/shard_map/dot_general | solution.py:121
  289.9 15.3 %convolution_convert_fusion.1 = bf16[1024,2048]{1,0:T(8,128)(2,1)} fusion(bf16[2048,2048]{1,0:T(8,128)(2,1)} %param.29, f32[1024,2048]{1,0:T(8,128)} %get-tuple-element.373, f32[2048]{0:T(1024)S(1)} %copy-done.73, f32[1024]{0:T(1024)S(1)} %add_rsqrt_fusion), kind=kOutput, calls=%fused_computation.140 | convolution fusion | flops 8598323200 | bytes 20983808 | tf_op jit(solution)/shard_map/dot_general | solution.py:150
  305.2 17.0 %multiply_reduce_fusion.2 = (f32[2048]{0:T(1024)}, f32[1024]{0:T(1024)S(1)}, f32[1024,2048]{1,0:T(8,128)}) fusion(f32[1024,2048]{1,0:T(8,128)} %get-tuple-element.373, f32[1024]{0:T(1024)S(1)} %add_rsqrt_fusion, f32[2048]{0:T(1024)S(1)} %copy-done.73, bf16[1024,2048]{1,0:T(8,128)(2,1)} %param.30, bf16[2048,2048]{1,0:T(8,128)(2,1)} %param.29), kind=kOutput, calls=%fused_computation.70 | convolution fusion | flops 8602514432 | bytes 29384704 | tf_op jit(solution)/shard_map/dot_general | solution.py:88
  327.2 20.5 %multiply_reduce_fusion.3 = (f32[2048]{0:T(1024)}, f32[1024,2048]{1,0:T(8,128)}, bf16[1024,2048]{1,0:T(8,128)(2,1)}) fusion(bf16[1024,2048]{1,0:T(8,128)(2,1)} %bitcast.262, f32[1024,2048]{1,0:T(8,128)} %get-tuple-element.413, f32[1024,2048]{1,0:T(8,128)} %get-tuple-element.373, f32[1024]{0:T(1024)S(1)} %fusion.141, f32[1024,2048]{1,0:T(8,128)} %get-tuple-element.414, ...), kind=kLoop, calls=%fused_computation.71 | loop fusion | flops 41940992 | bytes 50356224 | tf_op jit(solution)/shard_map/transpose(jvp())/reduce_sum | solution.py:69
  347.7 9.3 copy.163
  362.4 6.6 fusion.76
  369.1 12.3 %fusion.44 = f32[32,64,128,8]{2,3,1,0:T(8,128)S(1)} fusion(f32[8,32,64,128]{3,2,1,0:T(8,128)} %fusion.76, s32[8]{0:T(128)S(1)} %copy-done.51), kind=kOutput, calls=%fused_computation.68 | convolution fusion | flops 201326656 | bytes 16777248 | tf_op jit(solution)/shard_map/transpose(jvp(bq,qhpn->bhpn))/dot_general | solution.py:65
  381.4 9.7 convolution_bitcast_fusion.1
  391.1 21.3 %fusion.106 = f32[32,8,8]{2,1,0:T(8,128)S(1)} fusion(f32[32,64,128,8]{2,3,1,0:T(8,128)S(1)} %fusion.44, f32[8,32,64,128]{3,2,1,0:T(8,128)S(1)} %bitcast.259), kind=kOutput, calls=%fused_computation.159 | convolution fusion | flops 201326592 | bytes 16785408 | tf_op jit(solution)/shard_map/transpose(jvp(hba,ahpn->bhpn))/dot_general | solution.py:64
  412.5 6.8 multiply_reduce_fusion.9
  419.3 10.4 fusion.65
  429.7 18.2 %fusion.103 = f32[8,128,128]{2,1,0:T(8,128)S(1)} fusion(f32[8,32,64,128]{3,0,2,1:T(8,128)} %convolution_bitcast_fusion.1, f32[8,128,32]{1,2,0:T(8,128)S(1)} %copy-done.29, bf16[8,128,32,64]{1,0,3,2:T(8,128)(2,1)S(1)} %bitcast.266), kind=kOutput, calls=%fused_computation.156 | convolution fusion | flops 3225419776 | bytes 13238272 | tf_op jit(solution)/shard_map/transpose(jvp(bjh,bjhp,bjn->bhpn))/dot_general | solution.py:62
  448.0 15.7 %fusion.98 = f32[8,128,128]{2,1,0:T(8,128)S(1)} fusion(f32[8,32,64,128]{3,0,2,1:T(8,128)S(1)} %bitcast.257, f32[8,128,32,64]{1,0,3,2:T(8,128)S(1)} %bitcast.252, f32[8,128,32]{1,2,0:T(8,128)S(1)} %copy.148), kind=kOutput, calls=%fused_computation.155 | convolution fusion | flops 3223322624 | bytes 17432576 | tf_op jit(solution)/shard_map/transpose(jvp(bin,bhpn->bihp))/dot_general | solution.py:66
  463.8 28.9 %fusion.28 = (f32[8,128,32]{1,2,0:T(8,128)}, f32[8,128,32]{1,2,0:T(8,128)S(1)}, f32[8,128,32]{1,2,0:T(8,128)}, f32[8,128,128]{2,1,0:T(8,128)S(1)}) fusion(f32[8,128,32]{1,2,0:T(8,128)S(1)} %bitcast.299, f32[8,128,32]{1,2,0:T(8,128)S(1)} %copy-done.37, f32[8,128,128]{2,1,0:T(8,128)S(1)} %copy-done.31, pred[128,128]{1,0:T(8,128)(4,1)S(1)} %copy-done.64, ...), kind=kOutput, calls=%fused_computation.44 | convolution fusion | flops 3283910656 | bytes 14303232 | tf_op jit(solution)/shard_map/transpose(jvp(bijh,bjhp->bihp))/dot_general | solution.py:60
  497.8 10.7 multiply_reduce_fusion.1
  508.4 23.6 %bitcast_add_fusion = f32[8,128,32,64]{1,3,2,0:T(8,128)} fusion(f32[8,128,32,64]{1,3,2,0:T(8,128)} %fusion.65, f32[8,128,32,64]{1,0,3,2:T(8,128)S(1)} %bitcast.255, f32[32]{0:T(128)S(1)} %copy-done.91, f32[8,128,32]{1,2,0:T(8,128)S(1)} %copy-done.29, f32[8,128,32]{1,2,0:T(8,128)S(1)} %bitcast.300, f32[8,128,32]{1,2,0:T(8,128)S(1)} %copy-done.37, ...), kind=kOutput, calls=%fused_computation.58 | convolution fusion | flops 3250585600 | bytes 34488448 | tf_op jit(solution)/shard_map/transpose(jvp(bijh,bjhp->bihp))/dot_general | solution.py:60
  536.4 36.3 %while.31 = (s32[]{:T(128)}, f32[8,32]{1,0:T(8,128)}, f32[32,8,8]{2,1,0:T(8,128)S(1)}, f32[8,32,8,8]{3,2,1,0:T(8,128)}, s32[8]{0:T(128)}, /*index=5*/f32[8,32]{0...) while((s32[]{:T(128)}, f32[8,32]{1,0:T(8,128)}, f32[32,8,8]{2,1,0:T(8,128)S(1)}, ...), condition=%wide.region_15.16_spmd.clone, body=%wide.region_14.15_spmd.clone.sunk | while | flops 420484 | bytes 210855 | solution.py:39
  581.3 9.2 copy.170
  590.6 18.6 %multiply_reduce_fusion.6 = (f32[2048]{0:T(1024)}, f32[2048]{0:T(1024)}, f32[2048]{0:T(1024)}, f32[2048]{0:T(1024)}, f32[2048]{0:T(1024)}, /*index=5*/f32[8,128,2048]{2,1,0:T(8,128)S(1)}) fusion(f32[8,128,2048]{2,1,0:T(8,128)} %copy-done.7, f32[8,3,2048]{2,1,0:T(4,128)S(1)} %copy-done.19, f32[8,128,2048]{2,1,0:T(8,128)} %get-tuple-element.377, ...), kind=kLoop, calls=%fused_computation.74 | loop fusion | flops 44029952 | bytes 33792000 | tf_op jit(solution)/shard_map/transpose(jvp())/reduce_sum | solution.py:22
  609.2 11.9 %broadcast_multiply_fusion = (f32[8,128,2048]{2,1,0:T(8,128)}, f32[8,128,2048]{2,1,0:T(8,128)}, f32[8,128,2048]{2,1,0:T(8,128)}, f32[8,128,2048]{2,1,0:T(8,128)}) fusion(f32[8,128,2048]{2,1,0:T(8,128)S(1)} %get-tuple-element.366, f32[2048]{0:T(1024)S(1)} %bitcast.306, f32[2048]{0:T(1024)S(1)} %bitcast.304, f32[2048]{0:T(1024)S(1)} %bitcast.302, ...), kind=kLoop, calls=%fused_computation.136 | loop fusion | flops 8388608 | bytes 41975808 | tf_op jit(solution)/shard_map/transpose(jvp())/mul | solution.py:22
  629.6 13.1 %pad_add_fusion = f32[8,131,2048]{2,1,0:T(8,128)S(1)} fusion(f32[8,128,2048]{2,1,0:T(8,128)} %get-tuple-element.384, f32[8,128,2048]{2,1,0:T(8,128)} %get-tuple-element.385, f32[8,128,2048]{2,1,0:T(8,128)} %get-tuple-element.386, f32[8,128,2048]{2,1,0:T(8,128)} %get-tuple-element.383), kind=kLoop, calls=%fused_computation.42 | loop fusion | flops 6438912 | bytes 42139648 | tf_op jit(solution)/shard_map/transpose(jvp())/add_any | solution.py:22
  650.6 15.6 %fusion.87 = f32[1024,2048]{1,0:T(8,128)} fusion(bf16[1024,2048]{1,0:T(8,128)(2,1)S(1)} %copy-done.15, bf16[2048,1,2048]{2,1,0:T(2,128)(2,1)} %get-tuple-element.379), kind=kOutput, calls=%fused_computation.142 | convolution fusion | flops 8589934592 | bytes 20971520 | tf_op jit(solution)/shard_map/dot_general | solution.py:88
  666.2 24.1 %multiply_reduce_fusion.8 = (f32[2048]{0:T(1024)S(1)}, bf16[1024,2048]{1,0:T(8,128)(2,1)}, bf16[1024,2048]{1,0:T(8,128)(2,1)}) fusion(bf16[1024,2048]{1,0:T(8,128)(2,1)} %param.18, f32[1024]{0:T(1024)S(1)} %copy-done.59, bf16[1024,2048]{1,0:T(8,128)(2,1)} %all-reduce.29.cloned.1.call-done, f32[1024,2048]{1,0:T(8,128)} %fusion.138, ...), kind=kOutput, calls=%fused_computation.78 | convolution fusion | flops 8613001216 | bytes 54538240 | tf_op jit(solution)/shard_map/dot_general | solution.py:88
  694.5 15.3 %convolution_convert_fusion = bf16[2048,2048]{1,0:T(8,128)(2,1)} fusion(bf16[1024,2048]{1,0:T(8,128)(2,1)} %param.30, f32[1024,2048]{1,0:T(8,128)} %get-tuple-element.373, f32[2048]{0:T(1024)S(1)} %copy-done.74, f32[1024]{0:T(1024)S(1)} %copy-done.62), kind=kOutput, calls=%fused_computation.125 | convolution fusion | flops 8600420352 | bytes 20983808 | tf_op jit(solution)/shard_map/dot_general | solution.py:82
  709.7 12.4 %copy.213 = bf16[2048,2048]{0,1:T(8,128)(2,1)} copy(bf16[2048,2048]{1,0:T(8,128)(2,1)} %convolution_convert_fusion) | data formatting | bytes 16777216
  722.2 6.6 convert_element_type.94
  728.9 17.5 %reduce-scatter.9.cloned.1.call-done = bf16[512,2048]{1,0:T(8,128)(2,1)} async-done(((bf16[1024,2048]{1,0:T(8,128)(2,1)}), bf16[512,2048]{1,0:T(8,128)(2,1)}) %reduce-scatter.9.cloned.1.call-update) | async-done | bytes 2097168 | tf_op jit(solution)/shard_map/reduce_scatter | solution.py:181
  755.9 12.7 %convert_bitcast_fusion.1 = bf16[2048,1,2048]{2,0,1:T(8,128)(2,1)S(1)} fusion(bf16[1024,2048]{1,0:T(8,128)(2,1)} %copy-done.2, bf16[1024,2048]{1,0:T(8,128)(2,1)} %bitcast.285), kind=kOutput, calls=%fused_computation.76 | convolution fusion | flops 8594128896 | bytes 16777216 | tf_op jit(solution)/shard_map/dot_general | solution.py:82
  768.6 9.8 convert_bitcast_fusion.2
  778.4 6.8 pad_maximum_fusion
  790.7 63.7 %all-reduce.25 = (f32[5,2048]{1,0:T(8,128)}, f32[32]{0:T(128)}, f32[32]{0:T(128)}, f32[32]{0:T(128)}, f32[2048]{0:T(1024)}) all-reduce(f32[5,2048]{1,0:T(8,128)S(1)} %pad_add_fusion.3, f32[32]{0:T(128)S(1)} %get-tuple-element.364, f32[32]{0:T(128)S(1)} %negate_multiply_fusion, ...), channel_id=1, replica_groups=mesh['dp'=16,'tensor'=2] {'dp'}, use_global_device_ids=true, to_apply=%region_32.33 | all-reduce | flops 12384 | bytes 99072 | tf_op jit(solution)/shard_map/psum | solution.py:201
  855.9 39.0 %all-reduce.24 = (f32[2048]{0:T(1024)}, f32[5,256]{1,0:T(8,128)}) all-reduce(f32[2048]{0:T(1024)S(1)} %get-tuple-element.381, f32[5,256]{1,0:T(8,128)S(1)} %pad_add_fusion.4), channel_id=1, replica_groups=mesh['dp'=16,'tensor'=2] {'dp','tensor'}, use_global_device_ids=true, to_apply=%region_23.24 | all-reduce | flops 3328 | bytes 26624 | tf_op jit(solution)/shard_map/psum | solution.py:204
  894.8 22.0 %reduce-scatter.15.cloned.1.call-done = bf16[128,2048]{1,0:T(8,128)(2,1)} async-done(((bf16[2048,2048]{1,0:T(8,128)(2,1)}), bf16[128,2048]{1,0:T(8,128)(2,1)}) %reduce-scatter.15.cloned.1.call-update) | async-done | bytes 524304
  919.2 56.4 %all-gather.2.cloned.1.call-done = bf16[1024,2048]{1,0:T(8,128)(2,1)} async-done(((bf16[512,2048]{1,0:T(8,128)(2,1)}), bf16[1024,2048]{1,0:T(8,128)(2,1)}) %all-gather.2.cloned.1.call-update) | async-done | bytes 4194320 | tf_op jit(solution)/shard_map/all_gather | solution.py:189
  975.6 183.1 %reduce-scatter.11.cloned.1.call-done = bf16[128,2,2048]{2,0,1:T(8,128)(2,1)} async-done(((bf16[2048,2,2048]{2,0,1:T(8,128)(2,1)}), bf16[128,2,2048]{2,0,1:T(8,128)(2,1)}) %reduce-scatter.11.cloned.1.call-update) | async-done | bytes 1048592 | tf_op jit(solution)/shard_map/reduce_scatter | solution.py:191
  (395 shorter events, 176.5 us)
Async XLA Ops:
  8.0 137.2 %copy-start = (bf16[2048,256]{1,0:T(8,128)(2,1)S(1)}, bf16[2048,256]{1,0:T(8,128)(2,1)}, u32[]{:S(2)}) copy-start(bf16[2048,256]{1,0:T(8,128)(2,1)} %param.21) | copy-start | bytes 3145732
  8.0 658.2 %all-reduce.29.cloned.1.call-start = ((), (), s32[]{:S(2)}) async-start(), calls=%async_computation.4 | async-start | bytes 8388608 | tf_op jit(solution)/shard_map/psum | solution.py:155
  8.8 51.4 %copy-start.79 = (s32[8]{0:T(128)}, s32[8]{0:T(128)S(1)}, u32[]{:S(2)}) copy-start(s32[8]{0:T(128)S(1)} %broadcast_maximum_fusion) | copy-start | bytes 100
  9.5 139.9 %copy-start.76 = (pred[8]{0:T(512)(128)(4,1)}, pred[8]{0:T(512)(128)(4,1)S(1)}, u32[]{:S(2)}) copy-start(pred[8]{0:T(512)(128)(4,1)S(1)} %get-tuple-element.411) | copy-start | bytes 28
  12.6 32.9 %copy-start.58 = (f32[1024]{0:T(1024)}, f32[1024]{0:T(1024)S(1)}, u32[]{:S(2)}) copy-start(f32[1024]{0:T(1024)S(1)} %add_rsqrt_fusion.1) | copy-start | bytes 12292
  12.6 32.8 %copy-start.60 = (f32[5,2048]{1,0:T(8,128)S(1)}, f32[5,2048]{1,0:T(8,128)}, u32[]{:S(2)}) copy-start(f32[5,2048]{1,0:T(8,128)} %param.23) | copy-start | bytes 122884
  12.6 32.9 %copy-start.6 = (bf16[1024,2048]{1,0:T(8,128)(2,1)S(1)}, bf16[1024,2048]{1,0:T(8,128)(2,1)}, u32[]{:S(2)}) copy-start(bf16[1024,2048]{1,0:T(8,128)(2,1)} %param.18) | copy-start | bytes 12582916
  12.6 32.9 %copy-start.48 = (f32[2048]{0:T(1024)S(1)}, f32[2048]{0:T(1024)}, u32[]{:S(2)}) copy-start(f32[2048]{0:T(1024)} %param.19) | copy-start | bytes 24580
  45.5 18.8 %copy-start.40 = (f32[1,2048]{1,0:T(1,128)}, f32[1,2048]{1,0:T(1,128)S(1)}, u32[]{:S(2)}) copy-start(f32[1,2048]{1,0:T(1,128)S(1)} %get-tuple-element.402) | copy-start | bytes 24580
  45.5 18.8 %copy-start.42 = (f32[1,2048]{1,0:T(1,128)}, f32[1,2048]{1,0:T(1,128)S(1)}, u32[]{:S(2)}) copy-start(f32[1,2048]{1,0:T(1,128)S(1)} %get-tuple-element.403) | copy-start | bytes 24580
  45.5 18.8 %copy-start.44 = (f32[1,2048]{1,0:T(1,128)}, f32[1,2048]{1,0:T(1,128)S(1)}, u32[]{:S(2)}) copy-start(f32[1,2048]{1,0:T(1,128)S(1)} %get-tuple-element.404) | copy-start | bytes 24580
  45.5 18.8 %copy-start.46 = (f32[1,2048]{1,0:T(1,128)}, f32[1,2048]{1,0:T(1,128)S(1)}, u32[]{:S(2)}) copy-start(f32[1,2048]{1,0:T(1,128)S(1)} %get-tuple-element.405) | copy-start | bytes 24580
  93.9 35.0 %copy-start.51 = (s32[8]{0:T(128)S(1)}, s32[8]{0:T(128)}, u32[]{:S(2)}) copy-start(s32[8]{0:T(128)} %param.31) | copy-start | bytes 100
  100.4 29.3 %copy-start.88 = (f32[32]{0:T(128)}, f32[32]{0:T(128)S(1)}, u32[]{:S(2)}) copy-start(f32[32]{0:T(128)S(1)} %exponential_negate_fusion) | copy-start | bytes 388
  128.1 24.1 %copy-start.9 = (f32[8,128,32]{2,0,1:T(8,128)}, f32[8,128,32]{2,0,1:T(8,128)S(1)}, u32[]{:S(2)}) copy-start(f32[8,128,32]{2,0,1:T(8,128)S(1)} %fusion.171) | copy-start | bytes 393220
  128.2 24.1 %copy-start.50 = (f32[8,32]{1,0:T(8,128)}, f32[8,32]{1,0:T(8,128)S(1)}, u32[]{:S(2)}) copy-start(f32[8,32]{1,0:T(8,128)S(1)} %slice_bitcast_fusion) | copy-start | bytes 3076
  128.8 32.9 %copy-start.34 = (f32[8,8]{0,1:T(8,128)}, f32[8,8]{0,1:T(8,128)S(1)}, u32[]{:S(2)}) copy-start(f32[8,8]{0,1:T(8,128)S(1)} %fusion.143) | copy-start | bytes 772
  130.3 18.4 %copy-start.86 = (f32[5,256]{1,0:T(8,128)S(1)}, f32[5,256]{1,0:T(8,128)}, u32[]{:S(2)}) copy-start(f32[5,256]{1,0:T(8,128)} %param.24) | copy-start | bytes 15364
  155.6 22.9 %copy-start.28 = (f32[8,128,32]{1,2,0:T(8,128)}, f32[8,128,32]{1,2,0:T(8,128)S(1)}, u32[]{:S(2)}) copy-start(f32[8,128,32]{1,2,0:T(8,128)S(1)} %copy.150) | copy-start | bytes 393220
  170.9 21.2 %copy-start.22 = (f32[8,32]{0,1:T(8,128)}, f32[8,32]{0,1:T(8,128)S(1)}, u32[]{:S(2)}) copy-start(f32[8,32]{0,1:T(8,128)S(1)} %get-tuple-element.591) | copy-start | bytes 3076
  208.3 24.9 %copy-start.30 = (f32[8,128,128]{2,1,0:T(8,128)}, f32[8,128,128]{2,1,0:T(8,128)S(1)}, u32[]{:S(2)}) copy-start(f32[8,128,128]{2,1,0:T(8,128)S(1)} %fusion.173) | copy-start | bytes 1572868
  264.3 25.6 %copy-start.73 = (f32[2048]{0:T(1024)S(1)}, f32[2048]{0:T(1024)}, u32[]{:S(2)}) copy-start(f32[2048]{0:T(1024)} %param.28) | copy-start | bytes 24580
  289.8 37.3 %copy-start.61 = (f32[1024]{0:T(1024)}, f32[1024]{0:T(1024)S(1)}, u32[]{:S(2)}) copy-start(f32[1024]{0:T(1024)S(1)} %add_rsqrt_fusion) | copy-start | bytes 12292
  305.2 441.2 %reduce-scatter.9.cloned.1.call-start = ((), (), s32[]{:S(2)}) async-start(), calls=%async_computation.5 | async-start | bytes 6291456 | tf_op jit(solution)/shard_map/reduce_scatter | solution.py:181
  369.1 22.0 %slice-start.2 = ((s8[8388608]{0:T(1024)(128)(4,1)}), s8[4194304]{0:T(1024)(128)(4,1)S(1)}, s32[]{:S(2)}) async-start(s8[8388608]{0:T(1024)(128)(4,1)} %bitcast.258), calls=%async_computation.13 | async-start | bytes 8388608
  419.3 28.6 %slice-start = ((s8[8388608]{0:T(1024)(128)(4,1)}), s8[4194304]{0:T(1024)(128)(4,1)S(1)}, s32[]{:S(2)}) async-start(s8[8388608]{0:T(1024)(128)(4,1)} %bitcast.256), calls=%async_computation.11 | async-start | bytes 8388608
  429.7 18.2 %slice-start.1 = ((s8[8388608]{0:T(1024)(128)(4,1)}), s8[4194304]{0:T(1024)(128)(4,1)S(1)}, s32[]{:S(2)}) async-start(s8[8388608]{0:T(1024)(128)(4,1)} %bitcast.256), calls=%async_computation.12 | async-start | bytes 8388608
  463.7 30.0 %copy-start.12 = (f32[1024,256]{1,0:T(8,128)S(1)}, f32[1024,256]{1,0:T(8,128)}, u32[]{:S(2)}) copy-start(f32[1024,256]{1,0:T(8,128)} %copy-done.11) | copy-start | bytes 3145732
  463.7 30.0 %copy-start.17 = (f32[8,128,256]{2,1,0:T(8,128)S(1)}, f32[8,128,256]{2,1,0:T(8,128)}, u32[]{:S(2)}) copy-start(f32[8,128,256]{2,1,0:T(8,128)} %get-tuple-element.375) | copy-start | bytes 3145732
  463.7 30.0 %copy-start.33 = (f32[8,3,256]{2,1,0:T(4,128)S(1)}, f32[8,3,256]{2,1,0:T(4,128)}, u32[]{:S(2)}) copy-start(f32[8,3,256]{2,1,0:T(4,128)} %copy-done.32) | copy-start | bytes 73732
  508.4 28.0 %copy-start.23 = (f32[8,32]{0,1:T(8,128)S(1)}, f32[8,32]{0,1:T(8,128)}, u32[]{:S(2)}) copy-start(f32[8,32]{0,1:T(8,128)} %copy-done.22) | copy-start | bytes 3076
  532.1 40.7 %copy-start.10 = (f32[8,128,32]{2,0,1:T(8,128)S(1)}, f32[8,128,32]{2,0,1:T(8,128)}, u32[]{:S(2)}) copy-start(f32[8,128,32]{2,0,1:T(8,128)} %copy-done.9) | copy-start | bytes 393220
  532.1 43.3 %copy-start.13 = (f32[8,128,32]{2,0,1:T(8,128)S(1)}, f32[8,128,32]{2,0,1:T(8,128)}, u32[]{:S(2)}) copy-start(f32[8,128,32]{2,0,1:T(8,128)} %copy.149) | copy-start | bytes 393220
  590.5 18.6 %copy-start.41 = (f32[1,2048]{1,0:T(1,128)S(1)}, f32[1,2048]{1,0:T(1,128)}, u32[]{:S(2)}) copy-start(f32[1,2048]{1,0:T(1,128)} %copy-done.40) | copy-start | bytes 24580
  590.5 18.6 %copy-start.43 = (f32[1,2048]{1,0:T(1,128)S(1)}, f32[1,2048]{1,0:T(1,128)}, u32[]{:S(2)}) copy-start(f32[1,2048]{1,0:T(1,128)} %copy-done.42) | copy-start | bytes 24580
  590.5 18.6 %copy-start.45 = (f32[1,2048]{1,0:T(1,128)S(1)}, f32[1,2048]{1,0:T(1,128)}, u32[]{:S(2)}) copy-start(f32[1,2048]{1,0:T(1,128)} %copy-done.44) | copy-start | bytes 24580
  590.5 18.6 %copy-start.47 = (f32[1,2048]{1,0:T(1,128)S(1)}, f32[1,2048]{1,0:T(1,128)}, u32[]{:S(2)}) copy-start(f32[1,2048]{1,0:T(1,128)} %copy-done.46) | copy-start | bytes 24580
  690.3 164.1 %reduce-scatter.13.cloned.1.call-start = ((), (), s32[]{:S(2)}) async-start(), calls=%async_computation.9 | async-start | bytes 557056
  694.4 222.4 %reduce-scatter.15.cloned.1.call-start = ((), (), s32[]{:S(2)}) async-start(), calls=%async_computation.10 | async-start | bytes 8912896
  722.2 24.2 %copy-start.49 = (f32[2048]{0:T(1024)S(1)}, f32[2048]{0:T(1024)}, u32[]{:S(2)}) copy-start(f32[2048]{0:T(1024)} %param.19) | copy-start | bytes 24580
  722.2 253.4 %all-gather.2.cloned.1.call-start = ((), (), s32[]{:S(2)}) async-start(), calls=%async_computation.6 | async-start | bytes 6291456 | tf_op jit(solution)/shard_map/all_gather | solution.py:189
  755.8 402.9 %reduce-scatter.11.cloned.1.call-start = ((), (), s32[]{:S(2)}) async-start(), calls=%async_computation.7 | async-start | bytes 17825792 | tf_op jit(solution)/shard_map/reduce_scatter | solution.py:191
  785.4 69.0 %copy-start.81 = (f32[256]{0:T(256)S(1)}, f32[256]{0:T(256)}, u32[]{:S(2)}) copy-start(f32[256]{0:T(256)} %get-tuple-element.326) | copy-start | bytes 3076
  785.4 69.0 %copy-start.82 = (f32[256]{0:T(256)S(1)}, f32[256]{0:T(256)}, u32[]{:S(2)}) copy-start(f32[256]{0:T(256)} %get-tuple-element.327) | copy-start | bytes 3076
  785.4 69.0 %copy-start.83 = (f32[256]{0:T(256)S(1)}, f32[256]{0:T(256)}, u32[]{:S(2)}) copy-start(f32[256]{0:T(256)} %get-tuple-element.328) | copy-start | bytes 3076
  785.4 69.0 %copy-start.84 = (f32[256]{0:T(256)S(1)}, f32[256]{0:T(256)}, u32[]{:S(2)}) copy-start(f32[256]{0:T(256)} %get-tuple-element.329) | copy-start | bytes 3076
  785.4 69.0 %copy-start.85 = (f32[256]{0:T(256)S(1)}, f32[256]{0:T(256)}, u32[]{:S(2)}) copy-start(f32[256]{0:T(256)} %get-tuple-element.330) | copy-start | bytes 3076
  785.4 376.9 %all-reduce.31.cloned.1.call-start = ((), (), s32[]{:S(2)}) async-start(), calls=%async_computation.8 | async-start | bytes 4194304 | tf_op jit(solution)/shard_map/psum | solution.py:204
  (57 other events, 447.8 us)
Sparse Core Ops, SparseCore 0:
  305.3 109.7 all-reduce.28
  690.4 55.9 reduce-scatter.8
  750.5 56.5 reduce-scatter.12
  811.6 105.2 reduce-scatter.14
  918.9 56.6 all-gather.1
  980.1 178.5 reduce-scatter.10
Sparse Core Ops, SparseCore 1:
  792.7 204.7 all-reduce.30
where the time goes:
time: 1190 us; the launch traced here: 1180 us
  matrix products  397 us (33%)
  waiting for transfers between devices  279 us (23%)
  other arithmetic  188 us (16%)
  local copies, waits for them, and re-layouts  181 us (15%)
  blocking collectives  113 us (9%)
  between operations  17.5 us (1%)
    reduce_scatter x1, waiting for transfers between devices, local(): lax.psum_scatter(w_zx_part.astype(jnp.bfloat16), 'dp', scatter_dimension=...  183 us
    dot_general x3, matrix products, ssd_mix(): within = jnp.einsum('bijh,bjhp->bihp', weights, x_blocks, precision=highest)  74.5 us
    dot_general x5, matrix products, over_columns(): lax.dot_general(left, right, (((1,), (1,)), ((), ())), preferred_element_...  65.7 us
    psum x1, blocking collectives, local(): lax.psum((conv_x_part, dt_bias_part, a_log_part, d_skip_part, gate_gain_p...  63.7 us
    all_gather x1, waiting for transfers between devices, local(): lax.all_gather(d_input.astype(jnp.bfloat16), 'tensor', axis=0, tiled=True)  56.4 us
    dot_general x5, matrix products, over_tokens(): lax.dot_general(left, right, (((0,), (0,)), ((), ())), preferred_element_...  45.6 us
    dot_general x3, matrix products, ssd_mix(): jnp.einsum('hba,ahpn->bhpn', paths, local_states, precision=highest)  44.6 us
    unnamed x209, local copies, waits for them, and re-layouts  44.2 us
  transfers between devices with their start and end apart: 7, of which 4 were waited for; matrix products, arithmetic and copies ran while one was open for 38% of the time, Pallas kernels for 0%

commit v1 on v0

--- a/solution.py
+++ b/solution.py
@@ -1,10 +1,34 @@
+import functools
 import jax
 import jax.numpy as jnp
 from jax import lax
 from jax.sharding import PartitionSpec as P
+from jax.lax import axis_index, axis_size, ppermute
 
 epsilon = 1e-05
 highest = lax.Precision.HIGHEST
+
+
+def roads_try_all(frame_in, on_dim):
+    taken_in, z2, spare = (axis_size("tensor"), axis_index("tensor"), frame_in.shape[on_dim])
+    outcome_arr, b_now = (frame_in, 1)
+    while b_now < taken_in:
+        outcome_arr = jnp.concatenate(
+            [
+                outcome_arr,
+                ppermute(
+                    outcome_arr,
+                    "tensor",
+                    list(map(lambda no: (no, (no - b_now) % taken_in), range(taken_in))),
+                ),
+            ],
+            axis=on_dim,
+        )
+        b_now = 2 * b_now
+    return jnp.roll(outcome_arr, z2 * spare, axis=on_dim)
+
+
+extend_views = functools.partial(roads_try_all, on_dim=0)
 
 
 def conv_path(inputs, kernel, parent):
@@ -186,7 +210,7 @@
     gained = d_rows * norm_gain
     spread = rms_rows * rms_rows * rms_rows * jnp.sum(gained * x_rows, axis=-1) / features
     d_input = cot_rows + rms_rows[:, None] * gained - x_rows * spread[:, None]
-    input_grad = lax.all_gather(d_input.astype(jnp.bfloat16), "tensor", axis=0, tiled=True)
+    input_grad = extend_views(d_input.astype(jnp.bfloat16))
     w_zx_grad, w_dt_grad, w_out_grad = (
         lax.psum_scatter(
             w_zx_part.astype(jnp.bfloat16), "dp", scatter_dimension=0, tiled=True

time: 1190 us -> 1130 us (0.950)
  waiting for transfers between devices: 279 us -> 212 us
    all_gather x1 -> x0, waiting for transfers between devices: 56.4 us -> none  [local(): lax.all_gather(d_input.astype(jnp.bfloat16), 'tensor', axis=0, tiled=True)]
    unnamed x9 -> x8, waiting for transfers between devices: 22.1 us -> 43 us
    reduce_scatter x1, waiting for transfers between devices: 17.5 us -> 0.01 us  [local(): lax.psum_scatter(d_normed.astype(jnp.bfloat16), 'tensor', scatter_dimensi...]
    reduce_scatter x1, waiting for transfers between devices: 183 us -> 169 us  [local(): lax.psum_scatter(w_zx_part.astype(jnp.bfloat16), 'dp', scatter_dimension=...]
    unnamed x209 -> x212, local copies, waits for them, and re-layouts: 44.2 us -> 41.7 us
  transfers between devices with their start and end apart: 7 -> 7, of which waited for: 4 -> 2; matrix products, arithmetic and copies ran while one was open for 38% -> 41% of each run, Pallas kernels for 0% -> 0%
where the time goes in v1:
time: 1130 us; the launch traced here: 1110 us
  matrix products  395 us (35%)
  waiting for transfers between devices  212 us (19%)
  other arithmetic  197 us (17%)
  local copies, waits for them, and re-layouts  178 us (16%)
  blocking collectives  113 us (10%)
  between operations  17 us (2%)
    reduce_scatter x1, waiting for transfers between devices, local(): lax.psum_scatter(w_zx_part.astype(jnp.bfloat16), 'dp', scatter_dimension=...  169 us
    dot_general x3, matrix products, ssd_mix(): within = jnp.einsum('bijh,bjhp->bihp', weights, x_blocks, precision=highest)  74.5 us
    dot_general x5, matrix products, over_columns(): lax.dot_general(left, right, (((1,), (1,)), ((), ())), preferred_element_...  66 us
    psum x1, blocking collectives, local(): lax.psum((conv_x_part, dt_bias_part, a_log_part, d_skip_part, gate_gain_p...  62.2 us
    dot_general x3, matrix products, ssd_mix(): jnp.einsum('hba,ahpn->bhpn', paths, local_states, precision=highest)  44.6 us
    dot_general x5, matrix products, over_tokens(): lax.dot_general(left, right, (((0,), (0,)), ((), ())), preferred_element_...  43.2 us
    unnamed x8, waiting for transfers between devices  43 us
    unnamed x212, local copies, waits for them, and re-layouts  41.7 us
  transfers between devices with their start and end apart: 7, of which 2 were waited for; matrix products, arithmetic and copies ran while one was open for 41% of the time, Pallas kernels for 0%

profile of v1, /device:TPU:0, one launch (start us, length us, event | category | flops | bytes accessed | tf_op | source)
XLA Modules:
  0.0 1114.5 jit_solution(8363036324480666307)
XLA Ops:
  12.6 32.8 %fusion.168 = (bf16[2048,1,2048]{2,1,0:T(2,128)(2,1)}, bf16[2048,1,2048]{2,1,0:T(2,128)(2,1)}) fusion(bf16[2048,2,2048]{2,1,0:T(2,128)(2,1)} %param.20), kind=kLoop, calls=%fused_computation.261 | loop fusion | bytes 33554432 | tf_op jit(solution)/shard_map/slice | solution.py:145
  46.5 13.6 %fusion.40 = f32[8,128,2048]{2,1,0:T(8,128)S(1)} fusion(bf16[8,128,2048]{2,1,0:T(8,128)(2,1)S(1)} %bitcast.263, bf16[2048,1,2048]{2,1,0:T(2,128)(2,1)} %get-tuple-element.380), kind=kOutput, calls=%fused_computation.67 | convolution fusion | flops 8589934592 | bytes 20971520 | tf_op jit(solution)/shard_map/dot_general | solution.py:146
  64.3 16.3 %multiply_convert_fusion.1 = (bf16[8,128,2048]{2,1,0:T(8,128)(2,1)}, f32[8,128,2048]{2,1,0:T(8,128)}) fusion(f32[8,128,2048]{2,1,0:T(8,128)} %copy-done.8, f32[2048]{0:T(1024)S(1)} %bitcast.305, f32[8,3,2048]{2,1,0:T(4,128)S(1)} %select_select_fusion, f32[2048]{0:T(1024)S(1)} %bitcast.307, f32[2048]{0:T(1024)S(1)} %bitcast.301, f32[2048]{0:T(1024)S(1)} %bitcast.303, ...), kind=kLoop, calls=%fused_computation.105 | loop fusion | flops 33554432 | bytes 21209088 | tf_op jit(solution)/shard_map/convert_element_type | solution.py:118
  80.6 13.3 %reshape.279 = f32[8,128,32,64]{3,2,1,0:T(8,128)} reshape(bf16[1024,2048]{1,0:T(8,128)(2,1)} %bitcast.260) | data formatting | bytes 12582912 | tf_op jit(solution)/shard_map/jvp()/reshape;jvp()/reshape | solution.py:73
  93.9 6.4 copy.142
  104.8 23.3 %fusion.174 = f32[8,128,32]{2,0,1:T(8,128)S(1)} fusion(f32[8,128,32]{2,0,1:T(8,128)S(1)} %copy.143), kind=kOutput, calls=%fused_computation.267 | output fusion | flops 4161536 | bytes 262144 | tf_op jit(solution)/shard_map/jvp(jit(cumsum))/reduce_window_sum | solution.py:77
  130.3 14.6 %copy.158 = f32[8,128,32,64]{1,3,2,0:T(8,128)} copy(f32[8,128,32,64]{3,2,1,0:T(8,128)} %reshape.279) | data formatting | bytes 16777216 | tf_op jit(solution)/shard_map/jvp()/reshape;jvp()/reshape | solution.py:73
  161.5 9.1 while.30
  170.6 7.6 fusion.48
  178.3 13.7 %fusion.73 = f32[32,64,128,8]{2,3,1,0:T(8,128)S(1)} fusion(f32[8,32,64,128]{3,2,1,0:T(8,128)S(1)} %fusion.48, f32[32,8,8]{2,1,0:T(8,128)S(1)} %get-tuple-element.163), kind=kOutput, calls=%fused_computation.124 | convolution fusion | flops 201326592 | bytes 16785408 | tf_op jit(solution)/shard_map/jvp(hba,ahpn->bhpn)/dot_general | solution.py:88
  198.4 9.5 fusion.69
  211.2 21.9 %fusion.39 = f32[8,128,32,64]{1,3,2,0:T(8,128)} fusion(f32[8,128,32,64]{1,3,2,0:T(8,128)} %copy.158, f32[8,128,32,64]{1,3,2,0:T(8,128)S(1)} %fusion.69, f32[32]{0:T(128)S(1)} %copy-done.92, f32[8,128,32]{1,2,0:T(8,128)S(1)} %copy.148, f32[8,128,32]{1,2,0:T(8,128)S(1)} %bitcast.298, f32[8,128,32]{1,2,0:T(8,128)S(1)} %copy-done.38, ...), kind=kOutput, calls=%fused_computation.66 | convolution fusion | flops 3250585600 | bytes 30294144 | tf_op jit(solution)/shard_map/jvp(bijh,bjhp->bihp)/dot_general | solution.py:84
  233.2 16.2 %copy.215 = f32[8,128,32,64]{3,2,1,0:T(8,128)} copy(f32[8,128,32,64]{1,3,2,0:T(8,128)} %fusion.39) | data formatting | bytes 16777216 | tf_op jit(solution)/shard_map/jvp()/reshape | solution.py:94
  249.4 14.8 %reshape.284 = f32[1024,2048]{1,0:T(8,128)} reshape(f32[8,128,32,64]{3,2,1,0:T(8,128)} %copy.215) | data formatting | bytes 16777216 | tf_op jit(solution)/shard_map/jvp()/reshape | solution.py:94
  264.2 19.5 %multiply_reduce_fusion.11 = (f32[1024]{0:T(1024)S(1)}, f32[1024,2048]{1,0:T(8,128)}, f32[1024,2048]{1,0:T(8,128)}) fusion(f32[1024,2048]{1,0:T(8,128)} %reshape.284, bf16[1024,2048]{1,0:T(8,128)(2,1)} %copy-done.2, bf16[2048,1,2048]{2,1,0:T(2,128)(2,1)} %get-tuple-element.379), kind=kOutput, calls=%fused_computation.89 | convolution fusion | flops 8604613632 | bytes 37752832 | tf_op jit(solution)/shard_map/dot_general | solution.py:145
  289.6 15.3 %convolution_convert_fusion.1 = bf16[1024,2048]{1,0:T(8,128)(2,1)} fusion(bf16[2048,2048]{1,0:T(8,128)(2,1)} %param.29, f32[1024,2048]{1,0:T(8,128)} %get-tuple-element.373, f32[2048]{0:T(1024)S(1)} %copy-done.75, f32[1024]{0:T(1024)S(1)} %add_rsqrt_fusion), kind=kOutput, calls=%fused_computation.147 | convolution fusion | flops 8598323200 | bytes 20983808 | tf_op jit(solution)/shard_map/dot_general | solution.py:174
  304.9 17.0 %multiply_reduce_fusion.2 = (f32[2048]{0:T(1024)}, f32[1024]{0:T(1024)S(1)}, f32[1024,2048]{1,0:T(8,128)}) fusion(f32[1024,2048]{1,0:T(8,128)} %get-tuple-element.373, f32[1024]{0:T(1024)S(1)} %add_rsqrt_fusion, f32[2048]{0:T(1024)S(1)} %copy-done.75, bf16[1024,2048]{1,0:T(8,128)(2,1)} %param.30, bf16[2048,2048]{1,0:T(8,128)(2,1)} %param.29), kind=kOutput, calls=%fused_computation.74 | convolution fusion | flops 8602514432 | bytes 29384704 | tf_op jit(solution)/shard_map/dot_general | solution.py:112
  326.9 20.5 %multiply_reduce_fusion.3 = (f32[2048]{0:T(1024)}, f32[1024,2048]{1,0:T(8,128)}, bf16[1024,2048]{1,0:T(8,128)(2,1)}) fusion(bf16[1024,2048]{1,0:T(8,128)(2,1)} %bitcast.262, f32[1024,2048]{1,0:T(8,128)} %get-tuple-element.413, f32[1024,2048]{1,0:T(8,128)} %get-tuple-element.373, f32[1024]{0:T(1024)S(1)} %fusion.144, f32[1024,2048]{1,0:T(8,128)} %get-tuple-element.414, ...), kind=kLoop, calls=%fused_computation.75 | loop fusion | flops 41940992 | bytes 50356224 | tf_op jit(solution)/shard_map/transpose(jvp())/reduce_sum | solution.py:93
  347.5 9.3 copy.163
  362.2 6.6 fusion.76
  368.8 12.6 %fusion.44 = f32[32,64,128,8]{2,3,1,0:T(8,128)S(1)} fusion(f32[8,32,64,128]{3,2,1,0:T(8,128)} %fusion.76, s32[8]{0:T(128)S(1)} %copy-done.53), kind=kOutput, calls=%fused_computation.72 | convolution fusion | flops 201326656 | bytes 16777248 | tf_op jit(solution)/shard_map/transpose(jvp(bq,qhpn->bhpn))/dot_general | solution.py:89
  381.4 9.5 convolution_bitcast_fusion.1
  391.0 21.4 %fusion.109 = f32[32,8,8]{2,1,0:T(8,128)S(1)} fusion(f32[32,64,128,8]{2,3,1,0:T(8,128)S(1)} %fusion.44, f32[8,32,64,128]{3,2,1,0:T(8,128)S(1)} %bitcast.259), kind=kOutput, calls=%fused_computation.166 | convolution fusion | flops 201326592 | bytes 16785408 | tf_op jit(solution)/shard_map/transpose(jvp(hba,ahpn->bhpn))/dot_general | solution.py:88
  412.3 6.8 multiply_reduce_fusion.9
  419.1 10.4 fusion.65
  429.5 18.2 %fusion.106 = f32[8,128,128]{2,1,0:T(8,128)S(1)} fusion(f32[8,32,64,128]{3,0,2,1:T(8,128)} %convolution_bitcast_fusion.1, f32[8,128,32]{1,2,0:T(8,128)S(1)} %copy-done.31, bf16[8,128,32,64]{1,0,3,2:T(8,128)(2,1)S(1)} %bitcast.266), kind=kOutput, calls=%fused_computation.163 | convolution fusion | flops 3225419776 | bytes 13238272 | tf_op jit(solution)/shard_map/transpose(jvp(bjh,bjhp,bjn->bhpn))/dot_general | solution.py:86
  447.8 16.0 %fusion.101 = f32[8,128,128]{2,1,0:T(8,128)S(1)} fusion(f32[8,32,64,128]{3,0,2,1:T(8,128)S(1)} %bitcast.257, f32[8,128,32,64]{1,0,3,2:T(8,128)S(1)} %bitcast.252, f32[8,128,32]{1,2,0:T(8,128)S(1)} %copy.148), kind=kOutput, calls=%fused_computation.162 | convolution fusion | flops 3223322624 | bytes 17432576 | tf_op jit(solution)/shard_map/transpose(jvp(bin,bhpn->bihp))/dot_general | solution.py:90
  463.9 28.9 %fusion.28 = (f32[8,128,32]{1,2,0:T(8,128)}, f32[8,128,32]{1,2,0:T(8,128)S(1)}, f32[8,128,32]{1,2,0:T(8,128)}, f32[8,128,128]{2,1,0:T(8,128)S(1)}) fusion(f32[8,128,32]{1,2,0:T(8,128)S(1)} %bitcast.299, f32[8,128,32]{1,2,0:T(8,128)S(1)} %copy-done.39, f32[8,128,128]{2,1,0:T(8,128)S(1)} %copy-done.33, pred[128,128]{1,0:T(8,128)(4,1)S(1)} %copy-done.66, ...), kind=kOutput, calls=%fused_computation.44 | convolution fusion | flops 3283910656 | bytes 14303232 | tf_op jit(solution)/shard_map/transpose(jvp(bijh,bjhp->bihp))/dot_general | solution.py:84
  497.9 10.7 multiply_reduce_fusion.1
  508.5 23.6 %bitcast_add_fusion = f32[8,128,32,64]{1,3,2,0:T(8,128)} fusion(f32[8,128,32,64]{1,3,2,0:T(8,128)} %fusion.65, f32[8,128,32,64]{1,0,3,2:T(8,128)S(1)} %bitcast.255, f32[32]{0:T(128)S(1)} %copy-done.93, f32[8,128,32]{1,2,0:T(8,128)S(1)} %copy-done.31, f32[8,128,32]{1,2,0:T(8,128)S(1)} %bitcast.300, f32[8,128,32]{1,2,0:T(8,128)S(1)} %copy-done.39, ...), kind=kOutput, calls=%fused_computation.62 | convolution fusion | flops 3250585600 | bytes 34488448 | tf_op jit(solution)/shard_map/transpose(jvp(bijh,bjhp->bihp))/dot_general | solution.py:84
  536.5 36.3 %while.31 = (s32[]{:T(128)}, f32[8,32]{1,0:T(8,128)}, f32[32,8,8]{2,1,0:T(8,128)S(1)}, f32[8,32,8,8]{3,2,1,0:T(8,128)}, s32[8]{0:T(128)}, /*index=5*/f32[8,32]{0...) while((s32[]{:T(128)}, f32[8,32]{1,0:T(8,128)}, f32[32,8,8]{2,1,0:T(8,128)S(1)}, ...), condition=%wide.region_15.16_spmd.clone, body=%wide.region_14.15_spmd.clone.sunk | while | flops 420484 | bytes 210855 | solution.py:63
  581.3 9.2 copy.170
  590.6 18.6 %multiply_reduce_fusion.6 = (f32[2048]{0:T(1024)}, f32[2048]{0:T(1024)}, f32[2048]{0:T(1024)}, f32[2048]{0:T(1024)}, f32[2048]{0:T(1024)}, /*index=5*/f32[8,128,2048]{2,1,0:T(8,128)S(1)}) fusion(f32[8,128,2048]{2,1,0:T(8,128)} %copy-done.8, f32[8,3,2048]{2,1,0:T(4,128)S(1)} %copy-done.22, f32[8,128,2048]{2,1,0:T(8,128)} %get-tuple-element.377, ...), kind=kLoop, calls=%fused_computation.78 | loop fusion | flops 44029952 | bytes 33792000 | tf_op jit(solution)/shard_map/transpose(jvp())/reduce_sum | solution.py:46
  609.2 11.7 %broadcast_multiply_fusion = (f32[8,128,2048]{2,1,0:T(8,128)}, f32[8,128,2048]{2,1,0:T(8,128)}, f32[8,128,2048]{2,1,0:T(8,128)}, f32[8,128,2048]{2,1,0:T(8,128)}) fusion(f32[8,128,2048]{2,1,0:T(8,128)S(1)} %get-tuple-element.366, f32[2048]{0:T(1024)S(1)} %bitcast.306, f32[2048]{0:T(1024)S(1)} %bitcast.304, f32[2048]{0:T(1024)S(1)} %bitcast.302, ...), kind=kLoop, calls=%fused_computation.143 | loop fusion | flops 8388608 | bytes 41975808 | tf_op jit(solution)/shard_map/transpose(jvp())/mul | solution.py:46
  629.6 13.1 %pad_add_fusion = f32[8,131,2048]{2,1,0:T(8,128)S(1)} fusion(f32[8,128,2048]{2,1,0:T(8,128)} %get-tuple-element.384, f32[8,128,2048]{2,1,0:T(8,128)} %get-tuple-element.385, f32[8,128,2048]{2,1,0:T(8,128)} %get-tuple-element.386, f32[8,128,2048]{2,1,0:T(8,128)} %get-tuple-element.383), kind=kLoop, calls=%fused_computation.42 | loop fusion | flops 6438912 | bytes 42139648 | tf_op jit(solution)/shard_map/transpose(jvp())/add_any | solution.py:46
  650.6 15.9 %fusion.90 = f32[1024,2048]{1,0:T(8,128)} fusion(bf16[1024,2048]{1,0:T(8,128)(2,1)S(1)} %copy-done.16, bf16[2048,1,2048]{2,1,0:T(2,128)(2,1)} %get-tuple-element.379), kind=kOutput, calls=%fused_computation.149 | convolution fusion | flops 8589934592 | bytes 20971520 | tf_op jit(solution)/shard_map/dot_general | solution.py:112
  666.5 24.1 %multiply_reduce_fusion.8 = (f32[2048]{0:T(1024)S(1)}, bf16[1024,2048]{1,0:T(8,128)(2,1)}, bf16[1024,2048]{1,0:T(8,128)(2,1)}) fusion(bf16[1024,2048]{1,0:T(8,128)(2,1)} %param.18, f32[1024]{0:T(1024)S(1)} %copy-done.61, bf16[1024,2048]{1,0:T(8,128)(2,1)} %all-reduce.29.cloned.1.call-done, f32[1024,2048]{1,0:T(8,128)} %fusion.141, ...), kind=kOutput, calls=%fused_computation.82 | convolution fusion | flops 8613001216 | bytes 54538240 | tf_op jit(solution)/shard_map/dot_general | solution.py:112
  694.8 15.2 %convolution_convert_fusion = bf16[2048,2048]{1,0:T(8,128)(2,1)} fusion(bf16[1024,2048]{1,0:T(8,128)(2,1)} %param.30, f32[1024,2048]{1,0:T(8,128)} %get-tuple-element.373, f32[2048]{0:T(1024)S(1)} %copy-done.76, f32[1024]{0:T(1024)S(1)} %copy-done.64), kind=kOutput, calls=%fused_computation.129 | convolution fusion | flops 8600420352 | bytes 20983808 | tf_op jit(solution)/shard_map/dot_general | solution.py:106
  710.0 12.4 %copy.213 = bf16[2048,2048]{0,1:T(8,128)(2,1)} copy(bf16[2048,2048]{1,0:T(8,128)(2,1)} %convolution_convert_fusion) | data formatting | bytes 16777216
  722.5 12.5 %convert_bitcast_fusion.1 = bf16[2048,1,2048]{2,0,1:T(8,128)(2,1)S(1)} fusion(bf16[1024,2048]{1,0:T(8,128)(2,1)} %copy-done.2, bf16[1024,2048]{1,0:T(8,128)(2,1)} %bitcast.285), kind=kOutput, calls=%fused_computation.80 | convolution fusion | flops 8594128896 | bytes 16777216 | tf_op jit(solution)/shard_map/dot_general | solution.py:106
  735.0 9.8 convert_bitcast_fusion.2
  744.8 6.8 pad_maximum_fusion
  751.9 6.5 convert_element_type.94
  772.0 62.2 %all-reduce.25 = (f32[5,2048]{1,0:T(8,128)}, f32[32]{0:T(128)}, f32[32]{0:T(128)}, f32[32]{0:T(128)}, f32[2048]{0:T(1024)}) all-reduce(f32[5,2048]{1,0:T(8,128)S(1)} %pad_add_fusion.3, f32[32]{0:T(128)S(1)} %get-tuple-element.364, f32[32]{0:T(128)S(1)} %negate_multiply_fusion, ...), channel_id=1, replica_groups=mesh['dp'=16,'tensor'=2] {'dp'}, use_global_device_ids=true, to_apply=%region_32.33 | all-reduce | flops 12384 | bytes 99072 | tf_op jit(solution)/shard_map/psum | solution.py:225
  835.7 39.8 %all-reduce.24 = (f32[2048]{0:T(1024)}, f32[5,256]{1,0:T(8,128)}) all-reduce(f32[2048]{0:T(1024)S(1)} %get-tuple-element.381, f32[5,256]{1,0:T(8,128)S(1)} %pad_add_fusion.4), channel_id=1, replica_groups=mesh['dp'=16,'tensor'=2] {'dp','tensor'}, use_global_device_ids=true, to_apply=%region_23.24 | all-reduce | flops 3328 | bytes 26624 | tf_op jit(solution)/shard_map/psum | solution.py:228
  875.5 42.9 %reduce-scatter.15.cloned.1.call-done = bf16[128,2048]{1,0:T(8,128)(2,1)} async-done(((bf16[2048,2048]{1,0:T(8,128)(2,1)}), bf16[128,2048]{1,0:T(8,128)(2,1)}) %reduce-scatter.15.cloned.1.call-update) | async-done | bytes 524304
  922.5 9.4 fusion.84
  931.9 168.6 %reduce-scatter.11.cloned.1.call-done = bf16[128,2,2048]{2,0,1:T(8,128)(2,1)} async-done(((bf16[2048,2,2048]{2,0,1:T(8,128)(2,1)}), bf16[128,2,2048]{2,0,1:T(8,128)(2,1)}) %reduce-scatter.11.cloned.1.call-update) | async-done | bytes 1048592 | tf_op jit(solution)/shard_map/reduce_scatter | solution.py:215
  (398 shorter events, 167.7 us)
Async XLA Ops:
  8.0 136.9 %copy-start = (bf16[2048,256]{1,0:T(8,128)(2,1)S(1)}, bf16[2048,256]{1,0:T(8,128)(2,1)}, u32[]{:S(2)}) copy-start(bf16[2048,256]{1,0:T(8,128)(2,1)} %param.21) | copy-start | bytes 3145732
  8.0 658.5 %all-reduce.29.cloned.1.call-start = ((), (), s32[]{:S(2)}) async-start(), calls=%async_computation.4 | async-start | bytes 8388608 | tf_op jit(solution)/shard_map/psum | solution.py:179
  8.8 51.4 %copy-start.81 = (s32[8]{0:T(128)}, s32[8]{0:T(128)S(1)}, u32[]{:S(2)}) copy-start(s32[8]{0:T(128)S(1)} %broadcast_maximum_fusion) | copy-start | bytes 100
  9.5 139.6 %copy-start.78 = (pred[8]{0:T(512)(128)(4,1)}, pred[8]{0:T(512)(128)(4,1)S(1)}, u32[]{:S(2)}) copy-start(pred[8]{0:T(512)(128)(4,1)S(1)} %get-tuple-element.411) | copy-start | bytes 28
  12.6 32.9 %copy-start.60 = (f32[1024]{0:T(1024)}, f32[1024]{0:T(1024)S(1)}, u32[]{:S(2)}) copy-start(f32[1024]{0:T(1024)S(1)} %add_rsqrt_fusion.1) | copy-start | bytes 12292
  12.6 32.8 %copy-start.62 = (f32[5,2048]{1,0:T(8,128)S(1)}, f32[5,2048]{1,0:T(8,128)}, u32[]{:S(2)}) copy-start(f32[5,2048]{1,0:T(8,128)} %param.23) | copy-start | bytes 122884
  12.6 32.9 %copy-start.7 = (bf16[1024,2048]{1,0:T(8,128)(2,1)S(1)}, bf16[1024,2048]{1,0:T(8,128)(2,1)}, u32[]{:S(2)}) copy-start(bf16[1024,2048]{1,0:T(8,128)(2,1)} %param.18) | copy-start | bytes 12582916
  12.6 32.9 %copy-start.50 = (f32[2048]{0:T(1024)S(1)}, f32[2048]{0:T(1024)}, u32[]{:S(2)}) copy-start(f32[2048]{0:T(1024)} %param.19) | copy-start | bytes 24580
  45.5 18.8 %copy-start.42 = (f32[1,2048]{1,0:T(1,128)}, f32[1,2048]{1,0:T(1,128)S(1)}, u32[]{:S(2)}) copy-start(f32[1,2048]{1,0:T(1,128)S(1)} %get-tuple-element.402) | copy-start | bytes 24580
  45.5 18.8 %copy-start.44 = (f32[1,2048]{1,0:T(1,128)}, f32[1,2048]{1,0:T(1,128)S(1)}, u32[]{:S(2)}) copy-start(f32[1,2048]{1,0:T(1,128)S(1)} %get-tuple-element.403) | copy-start | bytes 24580
  45.5 18.8 %copy-start.46 = (f32[1,2048]{1,0:T(1,128)}, f32[1,2048]{1,0:T(1,128)S(1)}, u32[]{:S(2)}) copy-start(f32[1,2048]{1,0:T(1,128)S(1)} %get-tuple-element.404) | copy-start | bytes 24580
  45.5 18.8 %copy-start.48 = (f32[1,2048]{1,0:T(1,128)}, f32[1,2048]{1,0:T(1,128)S(1)}, u32[]{:S(2)}) copy-start(f32[1,2048]{1,0:T(1,128)S(1)} %get-tuple-element.405) | copy-start | bytes 24580
  93.9 35.0 %copy-start.53 = (s32[8]{0:T(128)S(1)}, s32[8]{0:T(128)}, u32[]{:S(2)}) copy-start(s32[8]{0:T(128)} %param.31) | copy-start | bytes 100
  100.4 29.3 %copy-start.90 = (f32[32]{0:T(128)}, f32[32]{0:T(128)S(1)}, u32[]{:S(2)}) copy-start(f32[32]{0:T(128)S(1)} %exponential_negate_fusion) | copy-start | bytes 388
  128.1 23.8 %copy-start.10 = (f32[8,128,32]{2,0,1:T(8,128)}, f32[8,128,32]{2,0,1:T(8,128)S(1)}, u32[]{:S(2)}) copy-start(f32[8,128,32]{2,0,1:T(8,128)S(1)} %fusion.174) | copy-start | bytes 393220
  128.2 23.8 %copy-start.52 = (f32[8,32]{1,0:T(8,128)}, f32[8,32]{1,0:T(8,128)S(1)}, u32[]{:S(2)}) copy-start(f32[8,32]{1,0:T(8,128)S(1)} %slice_bitcast_fusion) | copy-start | bytes 3076
  128.8 32.6 %copy-start.36 = (f32[8,8]{0,1:T(8,128)}, f32[8,8]{0,1:T(8,128)S(1)}, u32[]{:S(2)}) copy-start(f32[8,8]{0,1:T(8,128)S(1)} %fusion.146) | copy-start | bytes 772
  130.3 18.1 %copy-start.88 = (f32[5,256]{1,0:T(8,128)S(1)}, f32[5,256]{1,0:T(8,128)}, u32[]{:S(2)}) copy-start(f32[5,256]{1,0:T(8,128)} %param.24) | copy-start | bytes 15364
  155.4 22.9 %copy-start.30 = (f32[8,128,32]{1,2,0:T(8,128)}, f32[8,128,32]{1,2,0:T(8,128)S(1)}, u32[]{:S(2)}) copy-start(f32[8,128,32]{1,2,0:T(8,128)S(1)} %copy.150) | copy-start | bytes 393220
  170.6 21.4 %copy-start.24 = (f32[8,32]{0,1:T(8,128)}, f32[8,32]{0,1:T(8,128)S(1)}, u32[]{:S(2)}) copy-start(f32[8,32]{0,1:T(8,128)S(1)} %get-tuple-element.575) | copy-start | bytes 3076
  208.3 24.9 %copy-start.32 = (f32[8,128,128]{2,1,0:T(8,128)}, f32[8,128,128]{2,1,0:T(8,128)S(1)}, u32[]{:S(2)}) copy-start(f32[8,128,128]{2,1,0:T(8,128)S(1)} %fusion.176) | copy-start | bytes 1572868
  264.2 25.4 %copy-start.75 = (f32[2048]{0:T(1024)S(1)}, f32[2048]{0:T(1024)}, u32[]{:S(2)}) copy-start(f32[2048]{0:T(1024)} %param.28) | copy-start | bytes 24580
  289.6 37.4 %copy-start.63 = (f32[1024]{0:T(1024)}, f32[1024]{0:T(1024)S(1)}, u32[]{:S(2)}) copy-start(f32[1024]{0:T(1024)S(1)} %add_rsqrt_fusion) | copy-start | bytes 12292
  304.9 453.5 %reduce-scatter.9.cloned.1.call-start = ((), (), s32[]{:S(2)}) async-start(), calls=%async_computation.5 | async-start | bytes 6291456 | tf_op jit(solution)/shard_map/reduce_scatter | solution.py:205
  368.8 22.1 %slice-start.2 = ((s8[8388608]{0:T(1024)(128)(4,1)}), s8[4194304]{0:T(1024)(128)(4,1)S(1)}, s32[]{:S(2)}) async-start(s8[8388608]{0:T(1024)(128)(4,1)} %bitcast.258), calls=%async_computation.12 | async-start | bytes 8388608
  419.1 28.6 %slice-start = ((s8[8388608]{0:T(1024)(128)(4,1)}), s8[4194304]{0:T(1024)(128)(4,1)S(1)}, s32[]{:S(2)}) async-start(s8[8388608]{0:T(1024)(128)(4,1)} %bitcast.256), calls=%async_computation.10 | async-start | bytes 8388608
  429.5 18.3 %slice-start.1 = ((s8[8388608]{0:T(1024)(128)(4,1)}), s8[4194304]{0:T(1024)(128)(4,1)S(1)}, s32[]{:S(2)}) async-start(s8[8388608]{0:T(1024)(128)(4,1)} %bitcast.256), calls=%async_computation.11 | async-start | bytes 8388608
  463.8 30.0 %copy-start.13 = (f32[1024,256]{1,0:T(8,128)S(1)}, f32[1024,256]{1,0:T(8,128)}, u32[]{:S(2)}) copy-start(f32[1024,256]{1,0:T(8,128)} %copy-done.12) | copy-start | bytes 3145732
  463.8 30.0 %copy-start.18 = (f32[8,128,256]{2,1,0:T(8,128)S(1)}, f32[8,128,256]{2,1,0:T(8,128)}, u32[]{:S(2)}) copy-start(f32[8,128,256]{2,1,0:T(8,128)} %get-tuple-element.375) | copy-start | bytes 3145732
  463.8 30.0 %copy-start.35 = (f32[8,3,256]{2,1,0:T(4,128)S(1)}, f32[8,3,256]{2,1,0:T(4,128)}, u32[]{:S(2)}) copy-start(f32[8,3,256]{2,1,0:T(4,128)} %copy-done.34) | copy-start | bytes 73732
  508.5 28.0 %copy-start.25 = (f32[8,32]{0,1:T(8,128)S(1)}, f32[8,32]{0,1:T(8,128)}, u32[]{:S(2)}) copy-start(f32[8,32]{0,1:T(8,128)} %copy-done.24) | copy-start | bytes 3076
  532.1 40.7 %copy-start.11 = (f32[8,128,32]{2,0,1:T(8,128)S(1)}, f32[8,128,32]{2,0,1:T(8,128)}, u32[]{:S(2)}) copy-start(f32[8,128,32]{2,0,1:T(8,128)} %copy-done.10) | copy-start | bytes 393220
  532.1 43.3 %copy-start.14 = (f32[8,128,32]{2,0,1:T(8,128)S(1)}, f32[8,128,32]{2,0,1:T(8,128)}, u32[]{:S(2)}) copy-start(f32[8,128,32]{2,0,1:T(8,128)} %copy.149) | copy-start | bytes 393220
  590.6 18.6 %copy-start.43 = (f32[1,2048]{1,0:T(1,128)S(1)}, f32[1,2048]{1,0:T(1,128)}, u32[]{:S(2)}) copy-start(f32[1,2048]{1,0:T(1,128)} %copy-done.42) | copy-start | bytes 24580
  590.6 18.6 %copy-start.45 = (f32[1,2048]{1,0:T(1,128)S(1)}, f32[1,2048]{1,0:T(1,128)}, u32[]{:S(2)}) copy-start(f32[1,2048]{1,0:T(1,128)} %copy-done.44) | copy-start | bytes 24580
  590.6 18.6 %copy-start.47 = (f32[1,2048]{1,0:T(1,128)S(1)}, f32[1,2048]{1,0:T(1,128)}, u32[]{:S(2)}) copy-start(f32[1,2048]{1,0:T(1,128)} %copy-done.46) | copy-start | bytes 24580
  590.6 18.6 %copy-start.49 = (f32[1,2048]{1,0:T(1,128)S(1)}, f32[1,2048]{1,0:T(1,128)}, u32[]{:S(2)}) copy-start(f32[1,2048]{1,0:T(1,128)} %copy-done.48) | copy-start | bytes 24580
  621.9 20.8 %copy-start.19 = (bf16[8,128,256]{2,1,0:T(8,128)(2,1)}, bf16[8,128,256]{2,1,0:T(8,128)(2,1)S(1)}, u32[]{:S(2)}) copy-start(bf16[8,128,256]{2,1,0:T(8,128)(2,1)S(1)} %fusion.116) | copy-start | bytes 1572868
  690.6 143.6 %reduce-scatter.13.cloned.1.call-start = ((), (), s32[]{:S(2)}) async-start(), calls=%async_computation.8 | async-start | bytes 557056
  694.7 223.6 %reduce-scatter.15.cloned.1.call-start = ((), (), s32[]{:S(2)}) async-start(), calls=%async_computation.9 | async-start | bytes 8912896
  722.4 378.1 %reduce-scatter.11.cloned.1.call-start = ((), (), s32[]{:S(2)}) async-start(), calls=%async_computation.6 | async-start | bytes 17825792 | tf_op jit(solution)/shard_map/reduce_scatter | solution.py:215
  751.6 352.5 %all-reduce.31.cloned.1.call-start = ((), (), s32[]{:S(2)}) async-start(), calls=%async_computation.7 | async-start | bytes 4194304 | tf_op jit(solution)/shard_map/psum | solution.py:228
  762.2 71.9 %copy-start.83 = (f32[256]{0:T(256)S(1)}, f32[256]{0:T(256)}, u32[]{:S(2)}) copy-start(f32[256]{0:T(256)} %get-tuple-element.326) | copy-start | bytes 3076
  762.2 71.9 %copy-start.84 = (f32[256]{0:T(256)S(1)}, f32[256]{0:T(256)}, u32[]{:S(2)}) copy-start(f32[256]{0:T(256)} %get-tuple-element.327) | copy-start | bytes 3076
  762.2 71.9 %copy-start.85 = (f32[256]{0:T(256)S(1)}, f32[256]{0:T(256)}, u32[]{:S(2)}) copy-start(f32[256]{0:T(256)} %get-tuple-element.328) | copy-start | bytes 3076
  762.2 71.9 %copy-start.86 = (f32[256]{0:T(256)S(1)}, f32[256]{0:T(256)}, u32[]{:S(2)}) copy-start(f32[256]{0:T(256)} %get-tuple-element.329) | copy-start | bytes 3076
  762.3 71.9 %copy-start.87 = (f32[256]{0:T(256)S(1)}, f32[256]{0:T(256)}, u32[]{:S(2)}) copy-start(f32[256]{0:T(256)} %get-tuple-element.330) | copy-start | bytes 3076
  766.9 155.6 %collective-permute-start = (bf16[512,2048]{1,0:T(8,128)(2,1)S(1)}, bf16[512,2048]{1,0:T(8,128)(2,1)}, u32[]{:S(2)}, u32[]{:S(2)}) collective-permute-start(bf16[512,2048]{1,0:T(8,128)(2,1)S(1)} %subtract_convert_fusion), channel_id=1, source_target_pairs={{0,1},{1,0},{2,3},{3,2},{4,5},{5,4},{6,7},{7,6},{8,9},{9,8},{10,11... | collective-permute-start | bytes 6291464 | tf_op jit(solution)/shard_map/ppermute | solution.py:19
  (59 other events, 506.4 us)
Sparse Core Ops, SparseCore 0:
  305.0 109.7 all-reduce.28
  690.7 55.8 reduce-scatter.8
  750.8 56.7 reduce-scatter.12
  812.0 106.2 reduce-scatter.14
  922.9 177.5 reduce-scatter.10
Sparse Core Ops, SparseCore 1:
  771.7 166.6 all-reduce.30
